TPU v7x, 32 devices: a whole 2x2x4 slice. The times are simulated.
32 devices in a mesh: pipe: 8 (over y, x, core), sp: 4 (over z).
Axes of the slice: x: 2, y: 2, z: 4, core: 2. Of those that a mesh axis runs over, the one named last changes fastest.
Arguments:
- queries: bfloat16 [8, 512, 8192], P('pipe', 'sp'), may hold values from -48 to 48, as said below
- keys_values: bfloat16 [8, 512, 2048], P('pipe', 'sp'), may hold values from -8 to 8
- first_tile: int32 [8, 4], P('pipe'), may hold values from 0 to 3, as said below
Outputs:
- next_input: bfloat16 [8, 512, 8192], P('pipe', 'sp')
Inputs may be any that keep to these rules, and one draw needn't show every extreme that they name: queries[s, i, :] and keys_values[s, j, :] are of order one in most rows; a few rows are much larger. first_tile[s, t] is the first tile of the document that holds tile t of section s: first_tile[s, 0] = 0, first_tile[s, t] is t or first_tile[s, t - 1], and the last tile 4 - 1 begins a document.
All inputs are finite; a program needn't handle non-finite values.
Results may differ from a plain program's by a relative error of at most 0.0046.
Values may be sent and summed in bfloat16 or wider, within the bound.
A program may use at most 64 MiB of HBM per device.

v0:
```python
import math

import jax
import jax.numpy as jnp
from jax import lax
from jax.sharding import PartitionSpec as P

H = 64
KVH = 8
DH = 128
TILE = 128


def from_behind(block, axis, distance):
    devices = range(lax.axis_size(axis))
    route = [((i - distance) % len(devices), i) for i in devices]
    return lax.ppermute(block, axis, route)


def attend_heads(query_part, key_value_part, row_start):
    seq_len = query_part.shape[0]
    dim_head = query_part.shape[-1]
    block_rows = seq_len // 8
    scale_factor = 1.0 / math.sqrt(dim_head)
    key_part = key_value_part[..., :dim_head]
    value_part = key_value_part[..., dim_head:]
    pieces = []
    for block_index in range(8):
        begin_row = block_index * block_rows
        end_row = begin_row + block_rows
        scores = (
            jnp.einsum(
                "ikgd,jkd->kgij",
                query_part[begin_row:end_row],
                key_part[:end_row],
                preferred_element_type=jnp.float32,
            )
            * scale_factor
        )
        row_ids = jnp.arange(begin_row, end_row, dtype=jnp.int32)[:, None]
        col_ids = jnp.arange(end_row, dtype=jnp.int32)[None, :]
        visible = (col_ids <= row_ids) & (col_ids >= row_start[begin_row:end_row][:, None])
        scores = jnp.where(visible, scores, -jnp.inf)
        largest = jnp.max(scores, axis=-1, keepdims=True)
        exponent_terms = jnp.exp(scores - largest)
        weights = (exponent_terms / jnp.sum(exponent_terms, axis=-1, keepdims=True)).astype(
            jnp.bfloat16
        )
        attended = jnp.einsum(
            "kgij,jkd->ikgd", weights, value_part[:end_row], preferred_element_type=jnp.float32
        )
        pieces.append(attended.astype(jnp.bfloat16))
    return jnp.concatenate(pieces, axis=0)


def per_device(queries, keys_values, first_tile):
    section_queries = queries[0]
    section_kv = keys_values[0]
    token_count = section_queries.shape[0]
    shards = lax.axis_size("sp")
    local_heads = H // shards
    row_start = jnp.repeat(first_tile[0] * TILE, TILE)
    query_split = section_queries.reshape(token_count, shards, local_heads, DH)
    kv_heads = section_kv.reshape(token_count, KVH, 2 * DH)
    if KVH < shards:
        kv_heads = jnp.repeat(kv_heads, shards // KVH, axis=1)
    local_kv = kv_heads.shape[1] // shards
    kv_split = kv_heads.reshape(token_count, shards, local_kv, 2 * DH)
    query_heads, kv_local = (
        lax.all_to_all(query_split, "sp", split_axis=1, concat_axis=0, tiled=True),
        lax.all_to_all(kv_split, "sp", split_axis=1, concat_axis=0, tiled=True),
    )
    seq_len = query_heads.shape[0]
    outputs = attend_heads(
        query_heads.reshape(seq_len, local_kv, local_heads // local_kv, DH),
        kv_local.reshape(seq_len, local_kv, 2 * DH),
        row_start,
    )
    returned = lax.all_to_all(
        outputs.reshape(seq_len, 1, local_heads, DH), "sp", split_axis=0, concat_axis=1, tiled=True
    )
    result = from_behind(returned, "pipe", 1)
    return result.reshape(1, token_count, H * DH)


def solution(mesh):
    in_specs = (P("pipe", "sp", None), P("pipe", "sp", None), P("pipe", None))
    out_specs = P("pipe", "sp", None)
    return jax.shard_map(
        per_device, mesh=mesh, in_specs=in_specs, out_specs=out_specs, check_vma=False
    )
```

profile of v0, /device:TPU:8, one launch (start us, length us, event | category | flops | bytes accessed | tf_op | source)
XLA Modules:
  0.0 190.8 jit_solution(539952262099900849)
XLA Ops:
  0.0 1.3 copy.13
  2.3 5.3 %all-to-all-start = ((bf16[128,4,2,256]{3,0,2,1:T(8,128)(2,1)}), bf16[128,4,2,256]{3,0,2,1:T(8,128)(2,1)S(1)}, u32[]{:S(2)}, u32[]{:S(2)}) async-start(bf16[128,4,2,256]{3,0,2,1:T(8,128)(2,1)} %copy.14), calls=%async_computation | async-start | bytes 1048576 | tf_op jit(solution)/shard_map/all_to_all | solution.py:71
  7.6 3.2 %copy.16 = bf16[1,128,8192]{1,2,0:T(8,128)(2,1)S(1)} copy(bf16[1,128,8192]{2,1,0:T(8,128)(2,1)} %param.3) | data formatting | bytes 4194304 | tf_op args[0]
  10.9 2.6 %copy.17 = bf16[128,4,16,128]{3,0,2,1:T(8,128)(2,1)} copy(bf16[128,4,16,128]{0,3,2,1:T(8,128)(2,1)S(1)} %bitcast.277) | data formatting | bytes 4194304 | tf_op jit(solution)/shard_map/reshape;squeeze | solution.py:63
  13.5 5.4 %all-to-all-done = bf16[128,4,2,256]{3,0,2,1:T(8,128)(2,1)S(1)} async-done(((bf16[128,4,2,256]{3,0,2,1:T(8,128)(2,1)}), bf16[128,4,2,256]{3,0,2,1:T(8,128)(2,1)S(1)}, u32[]{:S(2)}, u32[]{:S(2)}) %all-to-all-start) | async-done | bytes 524320 | tf_op jit(solution)/shard_map/all_to_all | solution.py:71
  18.9 6.8 %all-to-all-start.1 = ((bf16[128,4,16,128]{3,0,2,1:T(8,128)(2,1)}), bf16[128,4,16,128]{3,0,2,1:T(8,128)(2,1)S(1)}, u32[]{:S(2)}, u32[]{:S(2)}) async-start(bf16[128,4,16,128]{3,0,2,1:T(8,128)(2,1)} %copy.17), calls=%async_computation.1 | async-start | bytes 4194304 | tf_op jit(solution)/shard_map/all_to_all | solution.py:70
  26.7 43.5 %all-to-all-done.1 = bf16[128,4,16,128]{3,0,2,1:T(8,128)(2,1)S(1)} async-done(((bf16[128,4,16,128]{3,0,2,1:T(8,128)(2,1)}), bf16[128,4,16,128]{3,0,2,1:T(8,128)(2,1)S(1)}, u32[]{:S(2)}, u32[]{:S(2)}) %all-to-all-start.1) | async-done | bytes 2097184 | tf_op jit(solution)/shard_map/all_to_all | solution.py:70
  70.3 1.3 copy-done
  72.0 1.5 fusion.157
  73.5 2.0 %fusion.29 = f32[2,8,64,128]{3,2,1,0:T(8,128)} fusion(bf16[512,2,8,128]{3,0,2,1:T(8,128)(2,1)} %bitcast.280, pred[64,128]{1,0:T(8,128)(4,1)S(1)} %fusion.97, bf16[512,2,256]{2,0,1:T(8,128)(2,1)S(1)} %bitcast.300), kind=kOutput, calls=%fused_computation.43 | convolution fusion | flops 33816576 | bytes 860160 | tf_op jit(solution)/shard_map/ikgd,jkd->kgij/dot_general | solution.py:32
  76.0 1.3 fusion.21
  77.9 1.3 fusion.19
  82.7 1.0 fusion.39
  83.7 3.7 %fusion.41 = bf16[512,2,8,128]{3,0,2,1:T(8,128)(2,1)} fusion(bf16[512,2,8,128]{3,0,2,1:T(8,128)(2,1)} %fusion.39, f32[2,8,64]{2,1,0:T(8,128)S(1)} %fusion.160, bf16[512,2,256]{2,0,1:T(8,128)(2,1)S(1)} %bitcast.311, f32[2,8,64,128]{3,2,1,0:T(8,128)} %fusion.29), kind=kOutput, calls=%fused_computation.63 | convolution fusion | flops 34079872 | bytes 1384448 | tf_op jit(solution)/shard_map/kgij,jkd->ikgd/dot_general | solution.py:49
  87.5 4.2 %fusion.35 = bf16[512,2,8,128]{3,0,2,1:T(8,128)(2,1)} fusion(bf16[512,2,8,128]{3,0,2,1:T(8,128)(2,1)} %fusion.41, f32[2,8,64]{2,1,0:T(8,128)S(1)} %fusion.163, f32[2,8,64,192]{3,2,1,0:T(8,128)} %fusion.21, bf16[512,2,256]{2,0,1:T(8,128)(2,1)S(1)} %bitcast.312), kind=kOutput, calls=%fused_computation.57 | convolution fusion | flops 51053760 | bytes 2465792 | tf_op jit(solution)/shard_map/kgij,jkd->ikgd/dot_general | solution.py:49
  91.6 4.3 %fusion.37 = bf16[512,2,8,128]{3,0,2,1:T(8,128)(2,1)} fusion(bf16[512,2,8,128]{3,0,2,1:T(8,128)(2,1)} %fusion.35, f32[2,8,64]{2,1,0:T(8,128)S(1)} %fusion.166, bf16[512,2,256]{2,0,1:T(8,128)(2,1)S(1)} %bitcast.313, f32[2,8,64,256]{3,2,1,0:T(8,128)} %fusion.19), kind=kOutput, calls=%fused_computation.59 | convolution fusion | flops 68027648 | bytes 2498560 | tf_op jit(solution)/shard_map/kgij,jkd->ikgd/dot_general | solution.py:49
  95.9 2.6 %fusion.31 = bf16[512,2,8,128]{3,0,2,1:T(8,128)(2,1)} fusion(bf16[512,2,8,128]{3,0,2,1:T(8,128)(2,1)} %fusion.37, f32[2,8,64]{2,1,0:T(8,128)S(1)} %fusion.169, bf16[512,2,256]{2,0,1:T(8,128)(2,1)S(1)} %bitcast.314, pred[64,320]{1,0:T(8,128)(4,1)S(1)} %fusion.80, bf16[512,2,8,128]{3,0,2,1:T(8,128)(2,1)S(1)} %bitcast.290), kind=kOutput, calls=%fused_computation.53 | convolution fusion | flops 169542976 | bytes 884736 | tf_op jit(solution)/shard_map/kgij,jkd->ikgd/dot_general | solution.py:49
  98.5 2.6 %fusion.33 = bf16[512,2,8,128]{3,0,2,1:T(8,128)(2,1)} fusion(bf16[512,2,8,128]{3,0,2,1:T(8,128)(2,1)} %fusion.31, f32[2,8,64]{2,1,0:T(8,128)S(1)} %fusion.172, bf16[512,2,256]{2,0,1:T(8,128)(2,1)S(1)} %bitcast.315, pred[64,384]{1,0:T(8,128)(4,1)S(1)} %fusion.81, bf16[512,2,8,128]{3,0,2,1:T(8,128)(2,1)S(1)} %bitcast.291), kind=kOutput, calls=%fused_computation.55 | convolution fusion | flops 203425152 | bytes 950272 | tf_op jit(solution)/shard_map/kgij,jkd->ikgd/dot_general | solution.py:49
  101.2 3.0 %fusion.43 = bf16[512,2,8,128]{3,0,2,1:T(8,128)(2,1)} fusion(bf16[512,2,8,128]{3,0,2,1:T(8,128)(2,1)} %fusion.33, f32[2,8,64]{2,1,0:T(8,128)S(1)} %fusion.175, bf16[512,2,256]{2,0,1:T(8,128)(2,1)S(1)} %bitcast.316, pred[64,448]{1,0:T(8,128)(4,1)S(1)} %fusion.78, bf16[512,2,8,128]{3,0,2,1:T(8,128)(2,1)S(1)} %bitcast.292), kind=kOutput, calls=%fused_computation.65 | convolution fusion | flops 237307328 | bytes 1024000 | tf_op jit(solution)/shard_map/kgij,jkd->ikgd/dot_general | solution.py:49
  104.1 2.8 %fusion.45 = bf16[512,2,8,128]{3,0,2,1:T(8,128)(2,1)} fusion(bf16[512,2,8,128]{3,0,2,1:T(8,128)(2,1)} %fusion.43, f32[2,8,64]{2,1,0:T(8,128)S(1)} %fusion.178, bf16[512,2,256]{2,0,1:T(8,128)(2,1)S(1)} %bitcast.317, pred[64,512]{1,0:T(8,128)(4,1)S(1)} %fusion.79, bf16[512,2,8,128]{3,0,2,1:T(8,128)(2,1)S(1)} %bitcast.293), kind=kOutput, calls=%fused_computation.67 | convolution fusion | flops 271189504 | bytes 1089536 | tf_op jit(solution)/shard_map/kgij,jkd->ikgd/dot_general | solution.py:49
  106.9 2.9 %copy.20 = bf16[512,1,16,128]{3,2,1,0:T(8,128)(2,1)S(1)} copy(bf16[512,1,16,128]{3,0,2,1:T(8,128)(2,1)} %bitcast.294) | data formatting | bytes 4194304 | tf_op jit(solution)/shard_map/reshape | solution.py:80
  109.8 51.7 %all_to_all.48 = bf16[512,1,16,128]{3,2,1,0:T(8,128)(2,1)S(1)} all-to-all(bf16[512,1,16,128]{3,2,1,0:T(8,128)(2,1)S(1)} %copy.20), channel_id=1, replica_groups=mesh['pipe'=8,'sp'=4] {'sp'}, dimensions={0} | all-to-all | bytes 4194304 | tf_op jit(solution)/shard_map/all_to_all | solution.py:79
  161.5 26.4 %collective-permute-done = bf16[128,4,16,128]{3,2,0,1:T(8,128)(2,1)S(1)} collective-permute-done((bf16[128,4,16,128]{3,2,0,1:T(8,128)(2,1)S(1)}, bf16[128,4,16,128]{3,2,0,1:T(8,128)(2,1)S(1)}, u32[]{:S(2)}, u32[]{:S(2)}) %collective-permute-start) | collective-permute-done | bytes 2097184 | tf_op jit(solution)/shard_map/ppermute | solution.py:17
  188.5 2.3 %reshape.75 = bf16[1,128,8192]{2,1,0:T(8,128)(2,1)} reshape(bf16[128,4,16,128]{3,2,1,0:T(8,128)(2,1)S(1)} %copy.21) | data formatting | bytes 4194304 | tf_op jit(solution)/shard_map/reshape | solution.py:83
  (36 shorter events, 7.5 us)
Async XLA Ops:
  2.3 16.6 %all-to-all-start = ((bf16[128,4,2,256]{3,0,2,1:T(8,128)(2,1)}), bf16[128,4,2,256]{3,0,2,1:T(8,128)(2,1)S(1)}, u32[]{:S(2)}, u32[]{:S(2)}) async-start(bf16[128,4,2,256]{3,0,2,1:T(8,128)(2,1)} %copy.14), calls=%async_computation | async-start | bytes 1048576 | tf_op jit(solution)/shard_map/all_to_all | solution.py:71
  13.5 12.3 %copy-start.2 = (s32[1,4]{1,0:T(1,128)S(1)}, s32[1,4]{1,0:T(1,128)}, u32[]{:S(2)}) copy-start(s32[1,4]{1,0:T(1,128)} %param.5) | copy-start | bytes 52
  18.9 51.2 %all-to-all-start.1 = ((bf16[128,4,16,128]{3,0,2,1:T(8,128)(2,1)}), bf16[128,4,16,128]{3,0,2,1:T(8,128)(2,1)S(1)}, u32[]{:S(2)}, u32[]{:S(2)}) async-start(bf16[128,4,16,128]{3,0,2,1:T(8,128)(2,1)} %copy.17), calls=%async_computation.1 | async-start | bytes 4194304 | tf_op jit(solution)/shard_map/all_to_all | solution.py:70
  70.3 1.3 copy-start
  72.0 3.5 %copy-start.1 = (bf16[4,128,1,16,128]{4,1,0,3,2:T(8,128)(2,1)S(1)}, bf16[4,128,1,16,128]{4,1,0,3,2:T(8,128)(2,1)}, u32[]{:S(2)}) copy-start(bf16[4,128,1,16,128]{4,1,0,3,2:T(8,128)(2,1)} %copy-done) | copy-start | bytes 6291460
  161.5 26.4 %collective-permute-start = (bf16[128,4,16,128]{3,2,0,1:T(8,128)(2,1)S(1)}, bf16[128,4,16,128]{3,2,0,1:T(8,128)(2,1)S(1)}, u32[]{:S(2)}, u32[]{:S(2)}) collective-permute-start(bf16[128,4,16,128]{3,2,0,1:T(8,128)(2,1)S(1)} %bitcast.295), channel_id=1, source_target_pairs={{28,0},{0,4},{4,8},{8,12},{12,16},{16,20},{20,24},{24,28},{29,1},{... | collective-permute-start | bytes 6291464 | tf_op jit(solution)/shard_map/ppermute | solution.py:17
where the time goes:
time: 194 us; the launch traced here: 191 us
  waiting for transfers between devices  75.3 us (39%)
  blocking collectives  51.7 us (27%)
  matrix products  35.2 us (18%)
  local copies, waits for them, and re-layouts  15.7 us (8%)
  starting transfers between devices  12.1 us (6%)
    all_to_all x1, blocking collectives, per_device(): lax.all_to_all(outputs.reshape(seq_len, 1, local_heads, DH), 'sp', split_...  51.7 us
    all_to_all x1, waiting for transfers between devices, per_device(): lax.all_to_all(query_split, 'sp', split_axis=1, concat_axis=0, tiled=True)  43.5 us
    ppermute x1, waiting for transfers between devices, from_behind(): return lax.ppermute(block, axis, route)  26.4 us
    dot_general x8, matrix products, attend_heads(): jnp.einsum('kgij,jkd->ikgd', weights, value_part[:end_row], preferred_ele...  24.2 us
    all_to_all x1, starting transfers between devices, per_device(): lax.all_to_all(query_split, 'sp', split_axis=1, concat_axis=0, tiled=True)  6.8 us
    sub x8, matrix products, attend_heads(): exponent_terms = jnp.exp(scores - largest)  6 us
    unnamed x8, local copies, waits for them, and re-layouts  5.84 us
    all_to_all x1, waiting for transfers between devices, per_device(): lax.all_to_all(kv_split, 'sp', split_axis=1, concat_axis=0, tiled=True)  5.44 us
  transfers between devices with their start and end apart: 3, of which 3 were waited for; matrix products, arithmetic and copies ran while one was open for 3% of the time, Pallas kernels for 0%

commit v1 on v0

v1 whole, which is shorter than its diff:
```python
import functools
import math

import jax
import jax.numpy as jnp
from jax import lax
from jax.experimental import pallas as pl
from jax.experimental.pallas import tpu as pltpu
from jax.sharding import PartitionSpec as P

H = 64
KVH = 8
DH = 128
REP = H // KVH
QW = REP * DH
KW = 2 * DH
UNROLL_TILES = 3
MESH = pl.DeviceIdType.MESH


def scores_of(query, key):
    return lax.dot_general(
        query, key, (((1,), (1,)), ((), ())), preferred_element_type=jnp.float32
    )


def kernel(n_pipe, n_sp, first_ref, q_hbm, kv_hbm, out_hbm, q_buf, own, kv_buf, staged,
           q_sem, own_sem, kv_send, kv_recv, out_send, out_recv):
    sp = lax.axis_index("sp")
    pipe = lax.axis_index("pipe")
    after = lax.rem(pipe + 1, n_pipe)
    before = lax.rem(pipe + n_pipe - 1, n_pipe)
    rows = q_buf.shape[0]
    last = n_sp - 1
    n_before = jnp.where(sp == last, 0, sp)

    def q_cols(g):
        return pl.ds(pl.multiple_of(g * QW, QW), QW)

    def kv_cols(g):
        return pl.ds(pl.multiple_of(g * KW, KW), KW)

    def q_copy(g):
        return pltpu.make_async_copy(q_hbm.at[0, :, q_cols(g)], q_buf.at[:, q_cols(g)], q_sem.at[g])

    def kv_copy(g, source, target):
        return pltpu.make_async_remote_copy(
            src_ref=kv_hbm.at[0, :, kv_cols(g)],
            dst_ref=kv_buf.at[source, :, kv_cols(g)],
            send_sem=kv_send.at[target, g],
            recv_sem=kv_recv.at[source, g],
            device_id={"sp": target},
            device_id_type=MESH,
        )

    def out_copy(g):
        return pltpu.make_async_remote_copy(
            src_ref=staged.at[:, q_cols(g)],
            dst_ref=out_hbm.at[0, :, q_cols(g)],
            send_sem=out_send.at[g],
            recv_sem=out_recv.at[g],
            device_id={"pipe": after},
            device_id_type=MESH,
        )

    barrier = pltpu.get_barrier_semaphore()
    for neighbour in (after, before):
        pl.semaphore_signal(barrier, inc=1, device_id={"pipe": neighbour}, device_id_type=MESH)
    for step in range(1, n_sp):
        pl.semaphore_signal(
            barrier, inc=1, device_id={"sp": lax.rem(sp + step, n_sp)}, device_id_type=MESH
        )
    own_copy = pltpu.make_async_copy(kv_hbm.at[0], own, own_sem)
    own_copy.start()
    for g in range(KVH):
        q_copy(g).start()
    pl.semaphore_wait(barrier, 2 + n_sp - 1)

    @pl.loop(0, KVH)
    def _(g):
        for target in range(last - 1, 0, -1):
            @pl.when(target > sp)
            def _():
                kv_copy(g, sp, target).start()

    own_copy.wait()
    first = first_ref[0, sp]
    factor = math.log2(math.e) / math.sqrt(DH)
    row_ids = lax.broadcasted_iota(jnp.int32, (rows, rows), 0)
    col_ids = lax.broadcasted_iota(jnp.int32, (rows, rows), 1)

    def bias_of(tile):
        return jnp.where(tile >= first, 0.0, -jnp.inf).astype(jnp.float32)

    def whole_softmax(g, count):
        k_cols = pl.ds(pl.multiple_of(g * KW, DH), DH)
        v_cols = pl.ds(pl.multiple_of(g * KW + DH, DH), DH)
        for head in range(REP):
            cols = pl.ds(pl.multiple_of(g * QW + head * DH, DH), DH)
            query = q_buf[:, cols]
            parts = [
                scores_of(query, kv_buf[tile, :, k_cols]) + bias_of(tile) for tile in range(count)
            ]
            parts.append(jnp.where(col_ids <= row_ids, scores_of(query, own[:, k_cols]), -jnp.inf))
            largest = jnp.max(functools.reduce(jnp.maximum, parts), axis=-1, keepdims=True)
            terms = [jnp.exp2((part - largest) * factor) for part in parts]
            total = jnp.sum(functools.reduce(jnp.add, terms), axis=-1, keepdims=True)
            share = 1.0 / total
            values = [kv_buf[tile, :, v_cols] for tile in range(count)] + [own[:, v_cols]]
            result = sum(
                jnp.dot((term * share).astype(jnp.bfloat16), value,
                        preferred_element_type=jnp.float32)
                for term, value in zip(terms, values)
            )
            staged[:, cols] = result.astype(jnp.bfloat16)

    def running_softmax(g):
        k_cols = pl.ds(pl.multiple_of(g * KW, DH), DH)
        v_cols = pl.ds(pl.multiple_of(g * KW + DH, DH), DH)

        @pl.loop(0, REP)
        def _(head):
            cols = pl.ds(pl.multiple_of(g * QW + head * DH, DH), DH)
            query = q_buf[:, cols]
            score = jnp.where(col_ids <= row_ids, scores_of(query, own[:, k_cols]), -jnp.inf)
            largest = jnp.max(score, axis=-1, keepdims=True)
            term = jnp.exp2((score - largest) * factor)
            total = jnp.sum(term, axis=-1, keepdims=True)
            result = jnp.dot(term.astype(jnp.bfloat16), own[:, v_cols],
                             preferred_element_type=jnp.float32)

            def step(tile, carry):
                largest, total, result = carry
                score = scores_of(query, kv_buf[tile, :, k_cols]) + bias_of(tile)
                larger = jnp.maximum(largest, jnp.max(score, axis=-1, keepdims=True))
                shrink = jnp.exp2((largest - larger) * factor)
                term = jnp.exp2((score - larger) * factor)
                total = total * shrink + jnp.sum(term, axis=-1, keepdims=True)
                result = result * shrink + jnp.dot(
                    term.astype(jnp.bfloat16), kv_buf[tile, :, v_cols],
                    preferred_element_type=jnp.float32)
                return larger, total, result

            _, total, result = lax.fori_loop(0, n_before, step, (largest, total, result))
            staged[:, cols] = (result / total).astype(jnp.bfloat16)

    @pl.loop(0, KVH)
    def _(g):
        q_copy(g).wait()
        for tile in range(last - 1):
            @pl.when(tile < n_before)
            def _():
                kv_copy(g, tile, sp).wait_recv()
        if last <= UNROLL_TILES:
            for count in range(max(last, 1)):
                @pl.when(n_before == count)
                def _():
                    whole_softmax(g, count)
        else:
            running_softmax(g)
        out_copy(g).start()

    @pl.loop(0, KVH)
    def _(g):
        for target in range(last - 1, 0, -1):
            @pl.when(target > sp)
            def _():
                kv_copy(g, sp, target).wait_send()
        out_copy(g).wait()


def per_device(n_pipe, n_sp, queries, keys_values, first_tile):
    rows = queries.shape[1]
    tiles = n_sp
    return pl.pallas_call(
        functools.partial(kernel, n_pipe, n_sp),
        out_shape=jax.ShapeDtypeStruct(queries.shape, jnp.bfloat16),
        in_specs=[
            pl.BlockSpec(memory_space=pltpu.SMEM),
            pl.BlockSpec(memory_space=pl.ANY),
            pl.BlockSpec(memory_space=pl.ANY),
        ],
        out_specs=pl.BlockSpec(memory_space=pl.ANY),
        scratch_shapes=[
            pltpu.VMEM((rows, H * DH), jnp.bfloat16),
            pltpu.VMEM((rows, KVH * KW), jnp.bfloat16),
            pltpu.VMEM((max(tiles - 2, 1), rows, KVH * KW), jnp.bfloat16),
            pltpu.VMEM((rows, H * DH), jnp.bfloat16),
            pltpu.SemaphoreType.DMA((KVH,)),
            pltpu.SemaphoreType.DMA,
            pltpu.SemaphoreType.DMA((tiles, KVH)),
            pltpu.SemaphoreType.DMA((tiles, KVH)),
            pltpu.SemaphoreType.DMA((KVH,)),
            pltpu.SemaphoreType.DMA((KVH,)),
        ],
        compiler_params=pltpu.CompilerParams(
            collective_id=0, has_side_effects=True, vmem_limit_bytes=40 * 1024 * 1024
        ),
    )(first_tile, queries, keys_values)


def solution(mesh):
    sizes = dict(mesh.shape)
    in_specs = (P("pipe", "sp", None), P("pipe", "sp", None), P("pipe", None))
    out_specs = P("pipe", "sp", None)
    return jax.shard_map(
        functools.partial(per_device, sizes["pipe"], sizes["sp"]),
        mesh=mesh, in_specs=in_specs, out_specs=out_specs, check_vma=False,
    )
```

time: 194 us -> 42.2 us (0.22)
  the two profiles are of different devices: /device:TPU:8 before, /device:TPU:16 now
where the time goes in v1:
time: 42.2 us; the launch traced here: 42 us
  Pallas kernels  37.4 us (89%)
  local copies, waits for them, and re-layouts  4.61 us (11%)
    pallas_call x1, Pallas kernels, per_device(): pl.pallas_call(functools.partial(kernel, n_pipe, n_sp), out_shape=jax.Sha...  37.4 us
    unnamed x7, local copies, waits for them, and re-layouts  4.61 us

profile of v1, /device:TPU:16, one launch (start us, length us, event | category | flops | bytes accessed | tf_op | source)
XLA Modules:
  0.0 42.0 jit_solution(15315077351291653216)
XLA Ops:
  0.0 0.0 copy-start
  0.0 1.6 %copy-done = bf16[1,128,8192]{2,1,0:T(8,128)(2,1)S(1)} copy-done((bf16[1,128,8192]{2,1,0:T(8,128)(2,1)S(1)}, bf16[1,128,8192]{2,1,0:T(8,128)(2,1)}, u32[]{:S(2)}) %copy-start) | copy-done | bytes 2097176
  1.6 0.0 copy-start.1
  1.6 1.0 %copy-done.1 = bf16[1,128,2048]{2,1,0:T(8,128)(2,1)S(1)} copy-done((bf16[1,128,2048]{2,1,0:T(8,128)(2,1)S(1)}, bf16[1,128,2048]{2,1,0:T(8,128)(2,1)}, u32[]{:S(2)}) %copy-start.1) | copy-done | bytes 524312
  2.6 0.0 copy-start.2
  2.6 0.7 %copy-done.2 = s32[1,4]{1,0:T(1,128)S(1)} copy-done((s32[1,4]{1,0:T(1,128)S(1)}, s32[1,4]{1,0:T(1,128)}, u32[]{:S(2)}) %copy-start.2) | copy-done | bytes 40
  3.3 37.4 %shard_map.37 = bf16[1,128,8192]{2,1,0:T(8,128)(2,1)S(1)} custom-call(s32[1,4]{1,0:T(1,128)S(1)} %copy-done.2, bf16[1,128,8192]{2,1,0:T(8,128)(2,1)S(1)} %copy-done, bf16[1,128,2048]{2,1,0:T(8,128)(2,1)S(1)} %copy-done.1), custom_call_target="tpu_custom_call" | custom-call | tf_op jit(solution)/shard_map/pallas_call | solution.py:175
  40.7 1.3 %copy.5 = bf16[1,128,8192]{2,1,0:T(8,128)(2,1)} copy(bf16[1,128,8192]{2,1,0:T(8,128)(2,1)S(1)} %shard_map.37) | data formatting | bytes 4194304
Async XLA Ops:
  0.0 1.6 %copy-start = (bf16[1,128,8192]{2,1,0:T(8,128)(2,1)S(1)}, bf16[1,128,8192]{2,1,0:T(8,128)(2,1)}, u32[]{:S(2)}) copy-start(bf16[1,128,8192]{2,1,0:T(8,128)(2,1)} %q_hbm.1) | copy-start | bytes 6291460
  1.6 1.0 %copy-start.1 = (bf16[1,128,2048]{2,1,0:T(8,128)(2,1)S(1)}, bf16[1,128,2048]{2,1,0:T(8,128)(2,1)}, u32[]{:S(2)}) copy-start(bf16[1,128,2048]{2,1,0:T(8,128)(2,1)} %kv_hbm.1) | copy-start | bytes 1572868
  2.6 0.7 %copy-start.2 = (s32[1,4]{1,0:T(1,128)S(1)}, s32[1,4]{1,0:T(1,128)}, u32[]{:S(2)}) copy-start(s32[1,4]{1,0:T(1,128)} %first_ref.1) | copy-start | bytes 52

commit v2 on v1

--- a/solution.py
+++ b/solution.py
@@ -15,6 +15,7 @@
 QW = REP * DH
 KW = 2 * DH
 UNROLL_TILES = 3
+STACK = 8
 MESH = pl.DeviceIdType.MESH
 
 
@@ -24,8 +25,8 @@
     )
 
 
-def kernel(n_pipe, n_sp, first_ref, q_hbm, kv_hbm, out_hbm, q_buf, own, kv_buf, staged,
-           q_sem, own_sem, kv_send, kv_recv, out_send, out_recv):
+def kernel(n_pipe, n_sp, first_hbm, q_hbm, kv_hbm, out_hbm, first_ref, q_buf, own, kv_buf, staged,
+           first_sem, q_sem, own_sem, kv_send, kv_recv, out_send, out_recv):
     sp = lax.axis_index("sp")
     pipe = lax.axis_index("pipe")
     after = lax.rem(pipe + 1, n_pipe)
@@ -72,6 +73,8 @@
         )
     own_copy = pltpu.make_async_copy(kv_hbm.at[0], own, own_sem)
     own_copy.start()
+    first_copy = pltpu.make_async_copy(first_hbm, first_ref, first_sem)
+    first_copy.start()
     for g in range(KVH):
         q_copy(g).start()
     pl.semaphore_wait(barrier, 2 + n_sp - 1)
@@ -84,6 +87,7 @@
                 kv_copy(g, sp, target).start()
 
     own_copy.wait()
+    first_copy.wait()
     first = first_ref[0, sp]
     factor = math.log2(math.e) / math.sqrt(DH)
     row_ids = lax.broadcasted_iota(jnp.int32, (rows, rows), 0)
@@ -95,13 +99,18 @@
     def whole_softmax(g, count):
         k_cols = pl.ds(pl.multiple_of(g * KW, DH), DH)
         v_cols = pl.ds(pl.multiple_of(g * KW + DH, DH), DH)
-        for head in range(REP):
-            cols = pl.ds(pl.multiple_of(g * QW + head * DH, DH), DH)
-            query = q_buf[:, cols]
+        for begin in range(0, REP, STACK):
+            cols = [
+                pl.ds(pl.multiple_of(g * QW + head * DH, DH), DH)
+                for head in range(begin, begin + STACK)
+            ]
+            query = jnp.concatenate([q_buf[:, c] for c in cols], axis=0)
             parts = [
                 scores_of(query, kv_buf[tile, :, k_cols]) + bias_of(tile) for tile in range(count)
             ]
-            parts.append(jnp.where(col_ids <= row_ids, scores_of(query, own[:, k_cols]), -jnp.inf))
+            score = scores_of(query, own[:, k_cols]).reshape(STACK, rows, rows)
+            score = jnp.where((col_ids <= row_ids)[None], score, -jnp.inf)
+            parts.append(score.reshape(STACK * rows, rows))
             largest = jnp.max(functools.reduce(jnp.maximum, parts), axis=-1, keepdims=True)
             terms = [jnp.exp2((part - largest) * factor) for part in parts]
             total = jnp.sum(functools.reduce(jnp.add, terms), axis=-1, keepdims=True)
@@ -111,8 +120,9 @@
                 jnp.dot((term * share).astype(jnp.bfloat16), value,
                         preferred_element_type=jnp.float32)
                 for term, value in zip(terms, values)
-            )
-            staged[:, cols] = result.astype(jnp.bfloat16)
+            ).astype(jnp.bfloat16)
+            for index, c in enumerate(cols):
+                staged[:, c] = result[index * rows:(index + 1) * rows]
 
     def running_softmax(g):
         k_cols = pl.ds(pl.multiple_of(g * KW, DH), DH)
@@ -176,16 +186,18 @@
         functools.partial(kernel, n_pipe, n_sp),
         out_shape=jax.ShapeDtypeStruct(queries.shape, jnp.bfloat16),
         in_specs=[
-            pl.BlockSpec(memory_space=pltpu.SMEM),
-            pl.BlockSpec(memory_space=pl.ANY),
-            pl.BlockSpec(memory_space=pl.ANY),
+            pl.BlockSpec(memory_space=pltpu.HBM),
+            pl.BlockSpec(memory_space=pltpu.HBM),
+            pl.BlockSpec(memory_space=pltpu.HBM),
         ],
         out_specs=pl.BlockSpec(memory_space=pl.ANY),
         scratch_shapes=[
+            pltpu.SMEM(first_tile.shape, jnp.int32),
             pltpu.VMEM((rows, H * DH), jnp.bfloat16),
             pltpu.VMEM((rows, KVH * KW), jnp.bfloat16),
             pltpu.VMEM((max(tiles - 2, 1), rows, KVH * KW), jnp.bfloat16),
             pltpu.VMEM((rows, H * DH), jnp.bfloat16),
+            pltpu.SemaphoreType.DMA,
             pltpu.SemaphoreType.DMA((KVH,)),
             pltpu.SemaphoreType.DMA,
             pltpu.SemaphoreType.DMA((tiles, KVH)),
@@ -196,7 +208,11 @@
         compiler_params=pltpu.CompilerParams(
             collective_id=0, has_side_effects=True, vmem_limit_bytes=40 * 1024 * 1024
         ),
-    )(first_tile, queries, keys_values)
+    )(
+        pltpu.with_memory_space_constraint(first_tile, pltpu.HBM),
+        pltpu.with_memory_space_constraint(queries, pltpu.HBM),
+        pltpu.with_memory_space_constraint(keys_values, pltpu.HBM),
+    )
 
 
 def solution(mesh):

time: 42.2 us -> 35.4 us (0.84)
  the two profiles are of different devices: /device:TPU:16 before, /device:TPU:8 now
where the time goes in v2:
time: 35.4 us; the launch traced here: 35.3 us
  Pallas kernels  34 us (96%)
  local copies, waits for them, and re-layouts  1.32 us (4%)
    pallas_call x1, Pallas kernels, per_device(): pl.pallas_call(functools.partial(kernel, n_pipe, n_sp), out_shape=jax.Sha...  34 us
    unnamed x1, local copies, waits for them, and re-layouts  1.32 us

profile of v2, /device:TPU:8, one launch (start us, length us, event | category | flops | bytes accessed | tf_op | source)
XLA Modules:
  0.0 35.3 jit_solution(1815328342122771756)
XLA Ops:
  0.0 34.0 %shard_map.37 = bf16[1,128,8192]{2,1,0:T(8,128)(2,1)S(1)} custom-call(s32[1,4]{1,0:T(1,128)} %first_hbm.1, bf16[1,128,8192]{2,1,0:T(8,128)(2,1)} %q_hbm.1, bf16[1,128,2048]{2,1,0:T(8,128)(2,1)} %kv_hbm.1), custom_call_target="tpu_custom_call" | custom-call | tf_op jit(solution)/shard_map/pallas_call | solution.py:185
  34.0 1.3 %copy.5 = bf16[1,128,8192]{2,1,0:T(8,128)(2,1)} copy(bf16[1,128,8192]{2,1,0:T(8,128)(2,1)S(1)} %shard_map.37) | data formatting | bytes 4194304

commit v3 on v2

--- a/solution.py
+++ b/solution.py
@@ -15,7 +15,10 @@
 QW = REP * DH
 KW = 2 * DH
 UNROLL_TILES = 3
-STACK = 8
+STACK = 4
+CHUNKS = REP // STACK
+CW = STACK * DH
+TURN_GROUP = 2
 MESH = pl.DeviceIdType.MESH
 
 
@@ -26,7 +29,7 @@
 
 
 def kernel(n_pipe, n_sp, first_hbm, q_hbm, kv_hbm, out_hbm, first_ref, q_buf, own, kv_buf, staged,
-           first_sem, q_sem, own_sem, kv_send, kv_recv, out_send, out_recv):
+           turn, first_sem, q_sem, own_sem, kv_send, kv_recv, out_send, out_recv):
     sp = lax.axis_index("sp")
     pipe = lax.axis_index("pipe")
     after = lax.rem(pipe + 1, n_pipe)
@@ -54,12 +57,13 @@
             device_id_type=MESH,
         )
 
-    def out_copy(g):
+    def out_copy(c):
+        cols = pl.ds(pl.multiple_of(c * CW, CW), CW)
         return pltpu.make_async_remote_copy(
-            src_ref=staged.at[:, q_cols(g)],
-            dst_ref=out_hbm.at[0, :, q_cols(g)],
-            send_sem=out_send.at[g],
-            recv_sem=out_recv.at[g],
+            src_ref=staged.at[:, cols],
+            dst_ref=out_hbm.at[0, :, cols],
+            send_sem=out_send.at[c],
+            recv_sem=out_recv.at[c],
             device_id={"pipe": after},
             device_id_type=MESH,
         )
@@ -67,17 +71,28 @@
     barrier = pltpu.get_barrier_semaphore()
     for neighbour in (after, before):
         pl.semaphore_signal(barrier, inc=1, device_id={"pipe": neighbour}, device_id_type=MESH)
-    for step in range(1, n_sp):
-        pl.semaphore_signal(
-            barrier, inc=1, device_id={"sp": lax.rem(sp + step, n_sp)}, device_id_type=MESH
-        )
+    for step in range(1, last):
+        @pl.when(sp < last)
+        def _():
+            pl.semaphore_signal(
+                barrier, inc=1, device_id={"sp": lax.rem(sp + step, last)}, device_id_type=MESH
+            )
     own_copy = pltpu.make_async_copy(kv_hbm.at[0], own, own_sem)
     own_copy.start()
     first_copy = pltpu.make_async_copy(first_hbm, first_ref, first_sem)
     first_copy.start()
     for g in range(KVH):
         q_copy(g).start()
-    pl.semaphore_wait(barrier, 2 + n_sp - 1)
+    pl.semaphore_wait(barrier, jnp.where(sp < last, last + 1, 2))
+
+    paired = n_pipe % 2 == 0
+    odd = lax.rem(pipe, 2) == 1
+    sends = sp < last - 1
+
+    if paired:
+        @pl.when(sends & jnp.logical_not(odd))
+        def _():
+            pl.semaphore_wait(turn, 1)
 
     @pl.loop(0, KVH)
     def _(g):
@@ -123,6 +138,7 @@
             ).astype(jnp.bfloat16)
             for index, c in enumerate(cols):
                 staged[:, c] = result[index * rows:(index + 1) * rows]
+            out_copy(g * CHUNKS + begin // STACK).start()
 
     def running_softmax(g):
         k_cols = pl.ds(pl.multiple_of(g * KW, DH), DH)
@@ -168,15 +184,27 @@
                     whole_softmax(g, count)
         else:
             running_softmax(g)
-        out_copy(g).start()
+            for chunk in range(CHUNKS):
+                out_copy(g * CHUNKS + chunk).start()
+        for target in range(last - 1, 0, -1):
+            @pl.when((target > sp) & odd)
+            def _():
+                kv_copy(g, sp, target).wait_send()
+        if paired:
+            @pl.when(sends & odd & (g == TURN_GROUP))
+            def _():
+                pl.semaphore_signal(
+                    turn, inc=1, device_id={"pipe": before}, device_id_type=MESH
+                )
 
     @pl.loop(0, KVH)
     def _(g):
         for target in range(last - 1, 0, -1):
-            @pl.when(target > sp)
+            @pl.when((target > sp) & jnp.logical_not(odd))
             def _():
                 kv_copy(g, sp, target).wait_send()
-        out_copy(g).wait()
+        for chunk in range(CHUNKS):
+            out_copy(g * CHUNKS + chunk).wait()
 
 
 def per_device(n_pipe, n_sp, queries, keys_values, first_tile):
@@ -197,13 +225,14 @@
             pltpu.VMEM((rows, KVH * KW), jnp.bfloat16),
             pltpu.VMEM((max(tiles - 2, 1), rows, KVH * KW), jnp.bfloat16),
             pltpu.VMEM((rows, H * DH), jnp.bfloat16),
+            pltpu.SemaphoreType.REGULAR,
             pltpu.SemaphoreType.DMA,
             pltpu.SemaphoreType.DMA((KVH,)),
             pltpu.SemaphoreType.DMA,
             pltpu.SemaphoreType.DMA((tiles, KVH)),
             pltpu.SemaphoreType.DMA((tiles, KVH)),
-            pltpu.SemaphoreType.DMA((KVH,)),
-            pltpu.SemaphoreType.DMA((KVH,)),
+            pltpu.SemaphoreType.DMA((KVH * CHUNKS,)),
+            pltpu.SemaphoreType.DMA((KVH * CHUNKS,)),
         ],
         compiler_params=pltpu.CompilerParams(
             collective_id=0, has_side_effects=True, vmem_limit_bytes=40 * 1024 * 1024

time: 35.4 us -> 33.7 us (0.952)
  Pallas kernels: 34 us -> 32.3 us
    pallas_call x1, Pallas kernels: 34 us -> 32.3 us  [per_device(): pl.pallas_call(functools.partial(kernel, n_pipe, n_sp), out_shape=jax.Sha...]
where the time goes in v3:
time: 33.7 us; the launch traced here: 33.6 us
  Pallas kernels  32.3 us (96%)
  local copies, waits for them, and re-layouts  1.32 us (4%)
    pallas_call x1, Pallas kernels, per_device(): pl.pallas_call(functools.partial(kernel, n_pipe, n_sp), out_shape=jax.Sha...  32.3 us
    unnamed x1, local copies, waits for them, and re-layouts  1.32 us

profile of v3, /device:TPU:8, one launch (start us, length us, event | category | flops | bytes accessed | tf_op | source)
XLA Modules:
  0.0 33.6 jit_solution(8991304039444025998)
XLA Ops:
  0.0 32.3 %shard_map.37 = bf16[1,128,8192]{2,1,0:T(8,128)(2,1)S(1)} custom-call(s32[1,4]{1,0:T(1,128)} %first_hbm.1, bf16[1,128,8192]{2,1,0:T(8,128)(2,1)} %q_hbm.1, bf16[1,128,2048]{2,1,0:T(8,128)(2,1)} %kv_hbm.1), custom_call_target="tpu_custom_call" | custom-call | tf_op jit(solution)/shard_map/pallas_call | solution.py:213
  32.3 1.3 %copy.5 = bf16[1,128,8192]{2,1,0:T(8,128)(2,1)} copy(bf16[1,128,8192]{2,1,0:T(8,128)(2,1)S(1)} %shard_map.37) | data formatting | bytes 4194304
